TPU v7x, 256 devices: a whole 4x4x8 slice. The times are simulated.
256 devices in a mesh: dp: 16 (over y_hi, z), mx: 8 (over x, core), my: 2 (over y_lo).
Axes of the slice: x: 4, y: 4 (y_hi: 2, y_lo: 2; y = y_hi * 2 + y_lo), z: 8, core: 2. Of those that a mesh axis runs over, the one named last changes fastest.
Arguments:
- inputs: bfloat16 [4096, 6144], P('dp', 'mx'), may hold values from -300 to 300
- ln_gain: float32 [6144], P('mx'), may hold values from 0.5 to 1.5
- w_qkv: bfloat16 [3, 6144, 4096], P(None, 'mx', 'my'), may hold values from -1 to 1
- qk_gain: float32 [2, 32, 128], P(None, ('my', 'mx')), may hold values from 0 to 8, as said below
- d_out: bfloat16 [4096, 4096], P('dp', ('my', 'mx')), may hold values from -110 to 110
Outputs:
- input_grad: bfloat16 [4096, 6144], P('dp', 'mx')
- w_grad: bfloat16 [3, 6144, 4096], P(None, ('mx', 'dp'), 'my')
- ln_gain_grad: float32 [6144], P('mx')
- qk_gain_grad: float32 [2, 32, 128], P(None, ('my', 'mx'))
Inputs may be any that keep to these rules, and one draw needn't show every extreme that they name: `qk_gain`: positive.
All inputs are finite; a program needn't handle non-finite values.
Results may differ from a plain program's by a relative error of at most 0.015.
The roundings to bfloat16 on the way count: a program that leaves them out, or rounds other values in their place, can miss the bound.
Values may be sent and summed in bfloat16 or wider, within the bound.
A program may use at most 128 MiB of HBM per device.

v0:
```python
import math
import jax
import jax.numpy as jnp
from jax import lax
from jax.sharding import PartitionSpec as P

PATCH = 256
epsilon = 1e-06


def head_norm(values):
    average = jnp.mean(values, axis=-1, keepdims=True)
    spread = jnp.mean(values * values, axis=-1, keepdims=True) - average * average
    inv_scale = lax.rsqrt(spread + epsilon)
    return ((values - average) * inv_scale, inv_scale)


def norm_back(d_normed, normed, inv_scale, gain_row):
    d_hat = d_normed * gain_row
    return inv_scale * (
        d_hat
        - jnp.mean(d_hat, axis=-1, keepdims=True)
        - normed * jnp.mean(d_hat * normed, axis=-1, keepdims=True)
    )


def body(inputs, ln_gain, w_qkv, qk_gain, d_out):
    token_rows = inputs.shape[0]
    width_local = inputs.shape[1]
    width = width_local * lax.axis_size("mx")
    widened = inputs.astype(jnp.float32)
    totals = lax.psum((jnp.sum(widened, axis=1), jnp.sum(widened * widened, axis=1)), "mx")
    average = totals[0][:, None] / width
    spread = totals[1][:, None] / width - average * average
    inv_scale = lax.rsqrt(spread + epsilon)
    normed = (widened - average) * inv_scale
    scaled = (normed * ln_gain[None, :]).astype(jnp.bfloat16)
    local_heads = qk_gain.shape[1]
    head_size = qk_gain.shape[2]
    group_heads = w_qkv.shape[2] // head_size
    weights = w_qkv.reshape(3, width_local, group_heads, head_size)
    projected = lax.psum_scatter(
        jnp.einsum("td,sdhe->hste", scaled, weights, preferred_element_type=jnp.float32),
        "mx",
        scatter_dimension=0,
        tiled=True,
    ).astype(jnp.bfloat16)
    images = token_rows // PATCH
    shaped = projected.reshape(local_heads, 3, images, PATCH, head_size)
    q_hat, q_inv = head_norm(shaped[:, 0].astype(jnp.float32))
    k_hat, k_inv = head_norm(shaped[:, 1].astype(jnp.float32))
    values = shaped[:, 2]
    q_gain = qk_gain[0][:, None, None, :]
    k_gain = qk_gain[1][:, None, None, :]
    q_normed = (q_hat * q_gain).astype(jnp.bfloat16)
    k_normed = (k_hat * k_gain).astype(jnp.bfloat16)
    factor = 1.0 / math.sqrt(head_size)
    scores = (
        jnp.einsum("hipe,hiqe->hipq", q_normed, k_normed, preferred_element_type=jnp.float32)
        * factor
    )
    row_max = jnp.max(scores, axis=-1, keepdims=True)
    exponent = jnp.exp(scores - row_max)
    probabilities = exponent / jnp.sum(exponent, axis=-1, keepdims=True)
    probs_low = probabilities.astype(jnp.bfloat16)
    grad_heads = (
        d_out.reshape(token_rows, local_heads, head_size)
        .transpose(1, 0, 2)
        .reshape(local_heads, images, PATCH, head_size)
    )
    d_values = jnp.einsum(
        "hipq,hipe->hiqe", probs_low, grad_heads, preferred_element_type=jnp.float32
    ).astype(jnp.bfloat16)
    d_probs = jnp.einsum("hipe,hiqe->hipq", grad_heads, values, preferred_element_type=jnp.float32)
    row_delta = jnp.sum(probabilities * d_probs, axis=-1, keepdims=True)
    d_scores = (probabilities * (d_probs - row_delta) * factor).astype(jnp.bfloat16)
    d_qn = jnp.einsum("hipq,hiqe->hipe", d_scores, k_normed, preferred_element_type=jnp.float32)
    d_kn = jnp.einsum("hipq,hipe->hiqe", d_scores, q_normed, preferred_element_type=jnp.float32)
    head_gain_part = jnp.stack(
        [jnp.sum(d_qn * q_hat, axis=(1, 2)), jnp.sum(d_kn * k_hat, axis=(1, 2))]
    )
    d_query = norm_back(d_qn, q_hat, q_inv, q_gain).astype(jnp.bfloat16)
    d_key = norm_back(d_kn, k_hat, k_inv, k_gain).astype(jnp.bfloat16)

    def head_rows(grads):
        return grads.reshape(local_heads, token_rows, head_size)

    block_rows = width_local // lax.axis_size("dp")
    stacked = jnp.stack([head_rows(d_query), head_rows(d_key), head_rows(d_values)], axis=1)
    gathered = lax.all_gather(stacked, "mx", axis=0, tiled=True)
    d_scaled = jnp.einsum("hste,sdhe->td", gathered, weights, preferred_element_type=jnp.float32)
    feature_part = scaled
    w_rows = lax.psum_scatter(
        jnp.einsum(
            "td,hste->dshe", feature_part, gathered, preferred_element_type=jnp.float32
        ).astype(jnp.bfloat16),
        "dp",
        scatter_dimension=0,
        tiled=True,
    ).astype(jnp.float32)
    w_grad = (
        w_rows.reshape(block_rows, 3, group_heads * head_size)
        .transpose(1, 0, 2)
        .astype(jnp.bfloat16)
    )
    gain_row = ln_gain[None, :]
    d_rows = lax.psum(d_scaled.astype(jnp.bfloat16), "my").astype(jnp.float32)
    d_hat = d_rows * gain_row
    stat_sums = lax.psum((jnp.sum(d_hat, axis=1), jnp.sum(d_hat * normed, axis=1)), "mx")
    sum_first = stat_sums[0]
    sum_second = stat_sums[1]
    result_rows = (
        inv_scale * (d_hat - sum_first[:, None] / width - normed * sum_second[:, None] / width)
    ).astype(jnp.bfloat16)
    feature_part = jnp.sum(d_rows * normed, axis=0)
    head_total, feature_total = lax.psum((head_gain_part, feature_part), "dp")
    return (result_rows, w_grad, feature_total, head_total)


def solution(mesh):
    in_specs = (
        P("dp", "mx"),
        P("mx"),
        P(None, "mx", "my"),
        P(None, ("my", "mx"), None),
        P("dp", ("my", "mx")),
    )
    out_specs = (P("dp", "mx"), P(None, ("mx", "dp"), "my"), P("mx"), P(None, ("my", "mx"), None))
    return jax.shard_map(body, mesh=mesh, in_specs=in_specs, out_specs=out_specs, check_vma=False)
```

profile of v0, /device:TPU:2, one launch (start us, length us, event | category | flops | bytes accessed | tf_op | source)
XLA Modules:
  0.0 439.1 jit_solution(7487721284132833700)
XLA Ops:
  7.2 0.0 copy-start
  7.2 0.0 all-gather.2.cloned.1.call-start
  7.2 0.7 slice_bitcast_fusion.3
  7.9 1.2 fusion.44
  9.1 11.7 %all-reduce.3 = (f32[256]{0:T(256)S(1)}, f32[256]{0:T(256)S(1)}) all-reduce(f32[256]{0:T(256)S(1)} %get-tuple-element.18, f32[256]{0:T(256)S(1)} %get-tuple-element.17), channel_id=1, replica_groups=mesh['dp'=16,'mx'=8,'my'=2] {'mx'}, use_global_device_ids=true, to_apply=%region_3.0 | all-reduce | flops 512 | bytes 4096 | tf_op jit(solution)/shard_map/psum | solution.py:32
  20.8 9.2 %fusion.10 = f32[16,3,256,128]{3,2,0,1:T(8,128)} fusion(bf16[256,768]{1,0:T(8,128)(2,1)} %param.5, f32[768]{0:T(1024)} %param.6, f32[256]{0:T(256)S(1)} %get-tuple-element.36, f32[256]{0:T(256)S(1)} %get-tuple-element.35, bf16[3,768,2048]{2,1,0:T(8,128)(2,1)} %param.7), kind=kOutput, calls=%fused_computation.11 | convolution fusion | flops 2416902144 | bytes 16126976 | tf_op jit(solution)/shard_map/td,sdhe->hste/dot_general | solution.py:43
  30.0 0.0 copy-start.5
  30.0 71.0 %all-reduce.8 = bf16[16,3,256,128]{3,2,0,1:T(8,128)(2,1)S(1)} all-reduce(f32[16,3,256,128]{3,2,0,1:T(8,128)} %fusion.10), channel_id=2, replica_groups=mesh['dp'=16,'mx'=8,'my'=2] {'mx'}, use_global_device_ids=true, to_apply=%region_4.0.clone | all-reduce | flops 1572864 | bytes 9437184
  101.0 0.0 copy-done.5
  101.0 0.6 dynamic-slice
  102.3 0.0 copy-start.2
  102.3 0.3 fusion.52
  102.6 0.4 copy-done.2
  103.1 0.0 copy-done
  103.1 0.2 convolution_bitcast_fusion
  103.3 0.0 copy-start.3
  103.3 1.6 fusion.109
  104.9 0.2 fusion.29
  105.2 1.3 fusion.30
  106.5 2.1 fusion.64
  108.6 0.0 copy-done.3
  108.6 0.6 fusion.84
  109.3 0.8 pad_maximum_fusion
  110.1 0.0 all-gather.2.cloned.1.call-update
  110.1 0.0 copy-start.1
  110.1 0.0 copy-start.4
  110.1 0.0 all-reduce.7.cloned.1.call-start
  110.2 33.7 %all-gather.2.cloned.1.call-done = bf16[16,3,256,128]{3,2,0,1:T(8,128)(2,1)} async-done(((bf16[2,3,256,128]{3,2,0,1:T(8,128)(2,1)}), bf16[16,3,256,128]{3,2,0,1:T(8,128)(2,1)}) %all-gather.2.cloned.1.call-update) | async-done | bytes 3145744 | tf_op jit(solution)/shard_map/all_gather | solution.py:90
  143.8 8.0 %fusion.19 = bf16[256,768]{1,0:T(8,128)(2,1)} fusion(bf16[16,3,256,128]{3,2,0,1:T(8,128)(2,1)} %all-gather.2.cloned.1.call-done, bf16[3,768,2048]{2,1,0:T(8,128)(2,1)} %param.7), kind=kOutput, calls=%fused_computation.14 | convolution fusion | flops 2416115712 | bytes 12976128 | tf_op jit(solution)/shard_map/hste,sdhe->td/dot_general | solution.py:91
  151.8 0.0 all-reduce.7.cloned.1.call-update
  151.8 0.2 reduce-scatter.5.cloned.1.call-start
  152.1 0.0 copy-done.1
  152.1 0.0 copy-done.4
  152.1 8.3 %convert_bitcast_fusion = bf16[768,3,16,128]{0,3,1,2:T(8,128)(2,1)} fusion(bf16[16,3,256,128]{3,2,0,1:T(8,128)(2,1)} %all-gather.2.cloned.1.call-done, bf16[256,768]{1,0:T(8,128)(2,1)S(1)} %copy-done.1, f32[768]{0:T(1024)S(1)} %copy-done.4, f32[256]{0:T(256)S(1)} %get-tuple-element.36, f32[256]{0:T(256)S(1)} %get-tuple-element.35), kind=kOutput, calls=%fused_computation.8 | convolution fusion | flops 2421620736 | bytes 12981248 | tf_op jit(solution)/shard_map/td,hste->dshe/dot_general | solution.py:94
  160.4 13.2 %copy.49 = bf16[768,3,16,128]{3,2,1,0:T(8,128)(2,1)} copy(bf16[768,3,16,128]{0,3,1,2:T(8,128)(2,1)} %convert_bitcast_fusion) | data formatting | bytes 18874368 | tf_op jit(solution)/shard_map/convert_element_type | solution.py:96
  173.6 0.0 reduce-scatter.5.cloned.1.call-update
  173.7 16.8 %all-reduce.7.cloned.1.call-done = bf16[256,768]{1,0:T(8,128)(2,1)} async-done(((bf16[256,768]{1,0:T(8,128)(2,1)}), bf16[256,768]{1,0:T(8,128)(2,1)}) %all-reduce.7.cloned.1.call-update) | async-done | bytes 393232 | tf_op jit(solution)/shard_map/psum | solution.py:107
  190.5 1.4 fusion.43
  191.9 11.5 %all-reduce.2 = (f32[256]{0:T(256)S(1)}, f32[256]{0:T(256)S(1)}) all-reduce(f32[256]{0:T(256)S(1)} %get-tuple-element.5, f32[256]{0:T(256)S(1)} %get-tuple-element.10), channel_id=1, replica_groups=mesh['dp'=16,'mx'=8,'my'=2] {'mx'}, use_global_device_ids=true, to_apply=%region_20.0 | all-reduce | flops 512 | bytes 4096 | tf_op jit(solution)/shard_map/psum | solution.py:109
  203.4 43.4 %all-reduce.1 = (f32[768]{0:T(1024)}, f32[2,2,128]{2,1,0:T(2,128)}) all-reduce(f32[768]{0:T(1024)S(1)} %get-tuple-element.4, f32[2,2,128]{2,1,0:T(2,128)S(1)} %pad_maximum_fusion.1), channel_id=1, replica_groups=mesh['dp'=16,'mx'=8,'my'=2] {'dp'}, use_global_device_ids=true, to_apply=%region_23.0 | all-reduce | flops 1280 | bytes 10240 | tf_op jit(solution)/shard_map/psum | solution.py:116
  246.8 2.1 fusion.41
  248.9 181.5 %reduce-scatter.5.cloned.1.call-done = bf16[48,3,16,128]{3,2,1,0:T(8,128)(2,1)} async-done(((bf16[768,3,16,128]{3,2,1,0:T(8,128)(2,1)}), bf16[48,3,16,128]{3,2,1,0:T(8,128)(2,1)}) %reduce-scatter.5.cloned.1.call-update) | async-done | bytes 589840 | tf_op jit(solution)/shard_map/reduce_scatter | solution.py:93
  430.4 1.2 copy.50
  431.6 1.1 convert_element_type.144
  (9 shorter events, 0.1 us)
Async XLA Ops:
  7.2 95.9 %copy-start = (bf16[256,256]{1,0:T(8,128)(2,1)S(1)}, bf16[256,256]{1,0:T(8,128)(2,1)}, u32[]{:S(2)}) copy-start(bf16[256,256]{1,0:T(8,128)(2,1)} %param.9) | copy-start | bytes 393220
  7.2 136.6 %all-gather.2.cloned.1.call-start = ((), (), s32[]{:S(2)}) async-start(), calls=%async_computation.1 | async-start | bytes 3538944 | tf_op jit(solution)/shard_map/all_gather | solution.py:90
  30.0 71.0 %copy-start.5 = (u32[256]{0:T(256)S(1)}, u32[256]{0:T(256)}, u32[]{:S(2)}) copy-start(u32[256]{0:T(256)} %constant.29) | copy-start | bytes 3076
  102.3 0.7 copy-start.2
  103.3 5.3 %copy-start.3 = (bf16[2,3,1,256,128]{4,3,0,2,1:T(8,128)(2,1)S(1)}, bf16[2,3,1,256,128]{4,3,0,2,1:T(8,128)(2,1)}, u32[]{:S(2)}) copy-start(bf16[2,3,1,256,128]{4,3,0,2,1:T(8,128)(2,1)} %copy-done.2) | copy-start | bytes 1179652
  110.1 42.0 %copy-start.1 = (bf16[256,768]{1,0:T(8,128)(2,1)S(1)}, bf16[256,768]{1,0:T(8,128)(2,1)}, u32[]{:S(2)}) copy-start(bf16[256,768]{1,0:T(8,128)(2,1)} %param.5) | copy-start | bytes 1179652
  110.1 42.0 %copy-start.4 = (f32[768]{0:T(1024)S(1)}, f32[768]{0:T(1024)}, u32[]{:S(2)}) copy-start(f32[768]{0:T(1024)} %param.6) | copy-start | bytes 9220
  110.1 80.4 %all-reduce.7.cloned.1.call-start = ((), (), s32[]{:S(2)}) async-start(), calls=%async_computation.2 | async-start | bytes 786432 | tf_op jit(solution)/shard_map/psum | solution.py:107
  151.8 278.5 %reduce-scatter.5.cloned.1.call-start = ((), (), s32[]{:S(2)}) async-start(), calls=%async_computation.3 | async-start | bytes 10027008 | tf_op jit(solution)/shard_map/reduce_scatter | solution.py:93
Sparse Core Ops, SparseCore 0:
  110.2 33.5 all-gather.1
  152.0 38.4 all-reduce.6
  194.7 235.6 reduce-scatter.4
where the time goes:
time: 440 us; the launch traced here: 439 us
  waiting for transfers between devices  232 us (53%)
  blocking collectives  138 us (31%)
  matrix products  31 us (7%)
  local copies, waits for them, and re-layouts  17.3 us (4%)
  between operations  14.6 us (3%)
  other arithmetic  6.45 us (1%)
    reduce_scatter x1, waiting for transfers between devices, body(): lax.psum_scatter(jnp.einsum('td,hste->dshe', feature_part, gathered, pref...  181 us
    unnamed x1, blocking collectives  71 us
    psum x1, blocking collectives, body(): head_total, feature_total = lax.psum((head_gain_part, feature_part), 'dp')  43.4 us
    all_gather x1, waiting for transfers between devices, body(): gathered = lax.all_gather(stacked, 'mx', axis=0, tiled=True)  33.7 us
    psum x1, waiting for transfers between devices, body(): d_rows = lax.psum(d_scaled.astype(jnp.bfloat16), 'my').astype(jnp.float32)  16.8 us
    convert_element_type x1, local copies, waits for them, and re-layouts, body(): w_rows = lax.psum_scatter(jnp.einsum('td,hste->dshe', feature_part, gathe...  13.2 us
    psum x1, blocking collectives, body(): lax.psum((jnp.sum(widened, axis=1), jnp.sum(widened * widened, axis=1)),...  11.7 us
    psum x1, blocking collectives, body(): lax.psum((jnp.sum(d_hat, axis=1), jnp.sum(d_hat * normed, axis=1)), 'mx')  11.5 us
  transfers between devices with their start and end apart: 3, of which 3 were waited for; matrix products, arithmetic and copies ran while one was open for 6% of the time, Pallas kernels for 0%

commit v1 on v0

--- a/solution.py
+++ b/solution.py
@@ -104,7 +104,11 @@
         .astype(jnp.bfloat16)
     )
     gain_row = ln_gain[None, :]
-    d_rows = lax.psum(d_scaled.astype(jnp.bfloat16), "my").astype(jnp.float32)
+    d_rows = (
+        jax.lax.all_gather(d_scaled.astype(jnp.bfloat16), axis_name="my")
+        .sum(axis=0)
+        .astype(jnp.float32)
+    )
     d_hat = d_rows * gain_row
     stat_sums = lax.psum((jnp.sum(d_hat, axis=1), jnp.sum(d_hat * normed, axis=1)), "mx")
     sum_first = stat_sums[0]

time: 440 us -> 414 us (0.941)
  waiting for transfers between devices: 232 us -> 193 us
  blocking collectives: 138 us -> 156 us
    reduce_scatter x1, waiting for transfers between devices: 181 us -> 159 us  [body(): lax.psum_scatter(jnp.einsum('td,hste->dshe', feature_part, gathered, pref...]
    all_gather x0 -> x1, blocking collectives: none -> 17.1 us  [body(): jax.lax.all_gather(d_scaled.astype(jnp.bfloat16), axis_name='my')]
    psum x1 -> x0, waiting for transfers between devices: 16.8 us -> none  [body(): d_rows = lax.psum(d_scaled.astype(jnp.bfloat16), 'my').astype(jnp.float32)]
  transfers between devices with their start and end apart: 3 -> 2, of which waited for: 3 -> 2; matrix products, arithmetic and copies ran while one was open for 6% -> 2% of each run, Pallas kernels for 0% -> 0%
where the time goes in v1:
time: 414 us; the launch traced here: 413 us
  waiting for transfers between devices  193 us (47%)
  blocking collectives  156 us (38%)
  matrix products  27.5 us (7%)
  local copies, waits for them, and re-layouts  17.8 us (4%)
  between operations  14.8 us (4%)
  other arithmetic  4.6 us (1%)
    reduce_scatter x1, waiting for transfers between devices, body(): lax.psum_scatter(jnp.einsum('td,hste->dshe', feature_part, gathered, pref...  159 us
    unnamed x1, blocking collectives  71.4 us
    psum x1, blocking collectives, body(): head_total, feature_total = lax.psum((head_gain_part, feature_part), 'dp')  44.1 us
    all_gather x1, waiting for transfers between devices, body(): gathered = lax.all_gather(stacked, 'mx', axis=0, tiled=True)  33.7 us
    all_gather x1, blocking collectives, body(): jax.lax.all_gather(d_scaled.astype(jnp.bfloat16), axis_name='my')  17.1 us
    convert_element_type x1, local copies, waits for them, and re-layouts, body(): w_rows = lax.psum_scatter(jnp.einsum('td,hste->dshe', feature_part, gathe...  13.2 us
    psum x1, blocking collectives, body(): lax.psum((jnp.sum(widened, axis=1), jnp.sum(widened * widened, axis=1)),...  11.7 us
    psum x1, blocking collectives, body(): lax.psum((jnp.sum(d_hat, axis=1), jnp.sum(d_hat * normed, axis=1)), 'mx')  11.4 us
  transfers between devices with their start and end apart: 2, of which 2 were waited for; matrix products, arithmetic and copies ran while one was open for 2% of the time, Pallas kernels for 0%

profile of v1, /device:TPU:2, one launch (start us, length us, event | category | flops | bytes accessed | tf_op | source)
XLA Modules:
  0.0 413.1 jit_solution(6711947171259365720)
XLA Ops:
  7.2 0.0 copy-start
  7.2 0.0 all-gather.3.cloned.1.call-start
  7.2 0.7 slice_bitcast_fusion.3
  7.9 1.2 fusion.44
  9.1 11.7 %all-reduce.3 = (f32[256]{0:T(256)S(1)}, f32[256]{0:T(256)S(1)}) all-reduce(f32[256]{0:T(256)S(1)} %get-tuple-element.18, f32[256]{0:T(256)S(1)} %get-tuple-element.17), channel_id=1, replica_groups=mesh['dp'=16,'mx'=8,'my'=2] {'mx'}, use_global_device_ids=true, to_apply=%region_3.0 | all-reduce | flops 512 | bytes 4096 | tf_op jit(solution)/shard_map/psum | solution.py:32
  20.8 9.2 %fusion.10 = f32[16,3,256,128]{3,2,0,1:T(8,128)} fusion(bf16[256,768]{1,0:T(8,128)(2,1)} %param.5, f32[768]{0:T(1024)} %param.6, f32[256]{0:T(256)S(1)} %get-tuple-element.36, f32[256]{0:T(256)S(1)} %get-tuple-element.35, bf16[3,768,2048]{2,1,0:T(8,128)(2,1)} %param.7), kind=kOutput, calls=%fused_computation.11 | convolution fusion | flops 2416902144 | bytes 16126976 | tf_op jit(solution)/shard_map/td,sdhe->hste/dot_general | solution.py:43
  30.0 0.0 copy-start.3
  30.0 71.4 %all-reduce.5 = bf16[16,3,256,128]{3,2,0,1:T(8,128)(2,1)} all-reduce(f32[16,3,256,128]{3,2,0,1:T(8,128)} %fusion.10), channel_id=3, replica_groups=mesh['dp'=16,'mx'=8,'my'=2] {'mx'}, use_global_device_ids=true, to_apply=%region_4.0.clone | all-reduce | flops 1572864 | bytes 9437184
  101.4 0.0 copy-start.1
  101.4 0.0 copy-start.2
  101.4 0.0 copy-done.3
  101.4 0.6 dynamic-slice
  102.6 1.0 fusion.50
  103.6 0.3 fusion.52
  103.9 0.0 copy-done
  103.9 0.2 convolution_bitcast_fusion
  104.2 0.8 fusion.109
  105.0 0.2 fusion.29
  105.2 0.4 fusion.30
  105.7 1.1 fusion.64
  106.8 0.6 fusion.84
  107.4 0.8 pad_maximum_fusion
  108.2 0.0 all-gather.3.cloned.1.call-update
  108.2 0.0 reduce-scatter.5.cloned.1.call-start
  108.3 33.7 %all-gather.3.cloned.1.call-done = bf16[16,3,256,128]{3,2,0,1:T(8,128)(2,1)} async-done(((bf16[2,3,256,128]{3,2,0,1:T(8,128)(2,1)}), bf16[16,3,256,128]{3,2,0,1:T(8,128)(2,1)}) %all-gather.3.cloned.1.call-update) | async-done | bytes 3145744 | tf_op jit(solution)/shard_map/all_gather | solution.py:90
  141.9 0.0 copy-done.1
  141.9 0.0 copy-done.2
  141.9 8.3 %convert_bitcast_fusion = bf16[768,3,16,128]{0,3,1,2:T(8,128)(2,1)} fusion(bf16[16,3,256,128]{3,2,0,1:T(8,128)(2,1)} %all-gather.3.cloned.1.call-done, bf16[256,768]{1,0:T(8,128)(2,1)S(1)} %copy-done.1, f32[768]{0:T(1024)S(1)} %copy-done.2, f32[256]{0:T(256)S(1)} %get-tuple-element.36, f32[256]{0:T(256)S(1)} %get-tuple-element.35), kind=kOutput, calls=%fused_computation.8 | convolution fusion | flops 2421620736 | bytes 12981248 | tf_op jit(solution)/shard_map/td,hste->dshe/dot_general | solution.py:94
  150.2 13.2 %copy.49 = bf16[768,3,16,128]{3,2,1,0:T(8,128)(2,1)} copy(bf16[768,3,16,128]{0,3,1,2:T(8,128)(2,1)} %convert_bitcast_fusion) | data formatting | bytes 18874368 | tf_op jit(solution)/shard_map/convert_element_type | solution.py:96
  163.5 0.0 reduce-scatter.5.cloned.1.call-update
  163.5 7.3 %fusion.19 = bf16[256,768]{1,0:T(8,128)(2,1)S(1)} fusion(bf16[16,3,256,128]{3,2,0,1:T(8,128)(2,1)} %all-gather.3.cloned.1.call-done, bf16[3,768,2048]{2,1,0:T(8,128)(2,1)} %param.7), kind=kOutput, calls=%fused_computation.14 | convolution fusion | flops 2416115712 | bytes 12976128 | tf_op jit(solution)/shard_map/hste,sdhe->td/dot_general | solution.py:91
  170.8 17.1 %all-gather = bf16[512,768]{1,0:T(8,128)(2,1)S(1)} all-gather(bf16[256,768]{1,0:T(8,128)(2,1)S(1)} %fusion.19), channel_id=2, replica_groups=mesh['dp'=16,'mx'=8,'my'=2] {'my'}, dimensions={0}, use_global_device_ids=true | all-gather | bytes 1179648 | tf_op jit(solution)/shard_map/all_gather | solution.py:108
  187.9 0.1 reduce_sum.177
  188.0 0.5 fusion.43
  188.5 11.4 %all-reduce.2 = (f32[256]{0:T(256)S(1)}, f32[256]{0:T(256)S(1)}) all-reduce(f32[256]{0:T(256)S(1)} %get-tuple-element.5, f32[256]{0:T(256)S(1)} %get-tuple-element.10), channel_id=1, replica_groups=mesh['dp'=16,'mx'=8,'my'=2] {'mx'}, use_global_device_ids=true, to_apply=%region_20.0 | all-reduce | flops 512 | bytes 4096 | tf_op jit(solution)/shard_map/psum | solution.py:113
  199.9 44.1 %all-reduce.1 = (f32[768]{0:T(1024)}, f32[2,2,128]{2,1,0:T(2,128)}) all-reduce(f32[768]{0:T(1024)S(1)} %get-tuple-element.4, f32[2,2,128]{2,1,0:T(2,128)S(1)} %pad_maximum_fusion.1), channel_id=1, replica_groups=mesh['dp'=16,'mx'=8,'my'=2] {'dp'}, use_global_device_ids=true, to_apply=%region_23.0 | all-reduce | flops 1280 | bytes 10240 | tf_op jit(solution)/shard_map/psum | solution.py:120
  244.0 1.1 fusion.41
  245.1 158.9 %reduce-scatter.5.cloned.1.call-done = bf16[48,3,16,128]{3,2,1,0:T(8,128)(2,1)} async-done(((bf16[768,3,16,128]{3,2,1,0:T(8,128)(2,1)}), bf16[48,3,16,128]{3,2,1,0:T(8,128)(2,1)}) %reduce-scatter.5.cloned.1.call-update) | async-done | bytes 589840 | tf_op jit(solution)/shard_map/reduce_scatter | solution.py:93
  404.0 1.2 copy.50
  405.2 1.1 convert_element_type.146
  (8 shorter events, 0.0 us)
Async XLA Ops:
  7.2 96.8 %copy-start = (bf16[256,256]{1,0:T(8,128)(2,1)S(1)}, bf16[256,256]{1,0:T(8,128)(2,1)}, u32[]{:S(2)}) copy-start(bf16[256,256]{1,0:T(8,128)(2,1)} %param.9) | copy-start | bytes 393220
  7.2 134.7 %all-gather.3.cloned.1.call-start = ((), (), s32[]{:S(2)}) async-start(), calls=%async_computation.1 | async-start | bytes 3538944 | tf_op jit(solution)/shard_map/all_gather | solution.py:90
  30.0 71.4 %copy-start.3 = (u32[256]{0:T(256)S(1)}, u32[256]{0:T(256)}, u32[]{:S(2)}) copy-start(u32[256]{0:T(256)} %constant.31) | copy-start | bytes 3076
  101.4 40.6 %copy-start.1 = (bf16[256,768]{1,0:T(8,128)(2,1)S(1)}, bf16[256,768]{1,0:T(8,128)(2,1)}, u32[]{:S(2)}) copy-start(bf16[256,768]{1,0:T(8,128)(2,1)} %param.5) | copy-start | bytes 1179652
  101.4 40.6 %copy-start.2 = (f32[768]{0:T(1024)S(1)}, f32[768]{0:T(1024)}, u32[]{:S(2)}) copy-start(f32[768]{0:T(1024)} %param.6) | copy-start | bytes 9220
  108.2 295.8 %reduce-scatter.5.cloned.1.call-start = ((), (), s32[]{:S(2)}) async-start(), calls=%async_computation.2 | async-start | bytes 10027008 | tf_op jit(solution)/shard_map/reduce_scatter | solution.py:93
Sparse Core Ops, SparseCore 0:
  108.3 33.5 all-gather.2
  163.6 240.3 reduce-scatter.4
